TPU v7x, 128 devices: a whole 4x4x4 slice. The times are simulated.
128 devices in a mesh: wide: 16 (over y, z), narrow: 8 (over x, core).
Axes of the slice: x: 4, y: 4, z: 4, core: 2. Of those that a mesh axis runs over, the one named last changes fastest.
Arguments:
- hidden_in: bfloat16 [1024, 7168], P(None, ('wide', 'narrow'))
- attn_gain: bfloat16 [7168], P(('wide', 'narrow')), may hold values from 0.099609375 to 1.8984375
- w_qkv: bfloat16 [7168, 8, 1152], P('wide', 'narrow'), may hold values from -0.0625 to 0.0625
- cache_kv: bfloat16 [2, 4096, 8, 2, 128], P(None, 'wide', 'narrow'), as said below
- lengths: int32 [2], replicated, may hold values from 1 to 4096, as said below
- offsets: int32 [2], replicated, may hold values from 0 to 4095
- w_out: bfloat16 [7168, 7168], P('narrow', 'wide'), may hold values from -0.0625 to 0.0625
- mlp_gain: bfloat16 [7168], P(('wide', 'narrow')), may hold values from 0.099609375 to 1.8984375
- w_gate_up: bfloat16 [7168, 2, 20480], P('wide', None, 'narrow'), may hold values from -0.0625 to 0.0625
- w_down: bfloat16 [20480, 7168], P('narrow', 'wide'), may hold values from -0.0390625 to 0.0390625
Outputs:
- hidden_out: bfloat16 [1024, 7168], P(None, ('wide', 'narrow'))
- softmax_sums: float32 [1024, 56], P('wide', 'narrow')
- new_cache: bfloat16 [1024, 8, 2, 128], P('wide', 'narrow')
Inputs may be any that keep to these rules, and one draw needn't show every extreme that they name: `lengths`: at least one request has all 4096 cached positions in use. `cache_kv`: positions at or beyond a request's length are never read.
All inputs are finite; a program needn't handle non-finite values.
Results may differ from a plain program's by a relative error of at most 0.01.
Values may be sent and summed in bfloat16 or wider, within the bound.
A program may use at most 192 MiB of HBM per device.

v0:
```python
import jax
import jax.numpy as jnp
from jax import lax
from jax.sharding import PartitionSpec as P

D = 7168
HDIM = 128
R = 2
GROUP = 7
epsilon = 1e-05
rope_base = 5000000.0
floor_score = -1e30


def norm_block(values, gain_vec):
    gathered, gain_row = (
        lax.all_gather(values, "narrow", axis=1, tiled=True),
        lax.all_gather(gain_vec.reshape(1, -1), "narrow", axis=1, tiled=True),
    )
    widened = gathered.astype(jnp.float32)
    squares = lax.psum(jnp.sum(widened * widened, axis=1), "wide")
    inv_scale = lax.rsqrt(squares / D + epsilon)
    return (widened * inv_scale[:, None] * gain_row.astype(jnp.float32)).astype(jnp.bfloat16)


def narrow_sums(partial_value):
    return lax.psum_scatter(partial_value, "narrow", scatter_dimension=1, tiled=True)


def token_angles(lengths, offsets, first_token, row_count, dim_size):
    token_ids = first_token + jnp.arange(row_count, dtype=jnp.int32)
    request_ids = token_ids % R
    start_pos = offsets + lengths
    matches = request_ids[:, None] == jnp.arange(start_pos.shape[0], dtype=jnp.int32)[None, :]
    chosen = jnp.sum(jnp.where(matches, start_pos[None, :], 0), axis=1)
    position = (chosen + token_ids // R).astype(jnp.float32)
    inverse = rope_base ** (-(jnp.arange(dim_size // 2, dtype=jnp.float32) * 2.0) / dim_size)
    return position[:, None] * inverse[None, :]


def rotate(values, angles):
    half_dim = values.shape[-1] // 2
    first_half = values[..., :half_dim]
    second_half = values[..., half_dim:]
    cosine = jnp.cos(angles)[:, None, :]
    sine_part = jnp.sin(angles)[:, None, :]
    return jnp.concatenate(
        [
            first_half * cosine - second_half * sine_part,
            second_half * cosine + first_half * sine_part,
        ],
        axis=-1,
    )


def absorb(running, scores, allowed, value_block, einsum_form):
    peak, weight_sum, accumulated = running
    scores = jnp.where(allowed, scores, floor_score)
    reduce_axes = tuple(range(3, scores.ndim))
    new_peak = jnp.maximum(peak, jnp.max(scores, axis=reduce_axes))
    expanded = new_peak.reshape(new_peak.shape + (1,) * len(reduce_axes))
    weights = jnp.where(allowed, jnp.exp(scores - expanded), 0.0)
    factor = jnp.exp(peak - new_peak)
    weight_sum = weight_sum * factor + jnp.sum(weights, axis=reduce_axes)
    accumulated = accumulated * factor[..., None] + jnp.einsum(
        einsum_form, weights.astype(jnp.bfloat16), value_block, preferred_element_type=jnp.float32
    )
    return (new_peak, weight_sum, accumulated)


def cache_step(running, remote, queries, request_ids, lengths):
    score_scale = HDIM ** (-0.5)
    scores = (
        jnp.einsum(
            "thgd,rphd->thgrp", queries, remote[:, :, :, 0], preferred_element_type=jnp.float32
        )
        * score_scale
    )
    position = jnp.arange(remote.shape[1], dtype=jnp.int32)
    usable = position[None, :] < lengths[:, None]
    owned = request_ids[:, None] == jnp.arange(lengths.shape[0], dtype=jnp.int32)[None, :]
    allowed = owned[:, None, None, :, None] & usable[None, None, None, :, :]
    return absorb(running, scores, allowed, remote[:, :, :, 1], "thgrp,rphd->thgd")


def start_state(row_count, heads_here):
    peak = jnp.full((row_count, heads_here, GROUP), floor_score, jnp.float32)
    weight_sum = jnp.zeros((row_count, heads_here, GROUP), jnp.float32)
    accumulated = jnp.zeros((row_count, heads_here, GROUP, HDIM), jnp.float32)
    return (peak, weight_sum, accumulated)


def local(
    hidden_in, attn_gain, w_qkv, cache_kv, lengths, offsets, w_out, mlp_gain, w_gate_up, w_down
):
    all_tokens = hidden_in.shape[0]
    per_device = all_tokens // lax.axis_size("wide")
    first_token = lax.axis_index("wide") * per_device
    heads_here = w_qkv.shape[1]
    score_scale = HDIM ** (-0.5)
    normed = norm_block(hidden_in, attn_gain)
    flat_qkv = w_qkv.reshape(w_qkv.shape[0], -1)
    row_block = normed
    projected = lax.psum_scatter(
        jnp.dot(row_block, flat_qkv, preferred_element_type=jnp.float32),
        "wide",
        scatter_dimension=0,
        tiled=True,
    )
    projected = projected.reshape(per_device, heads_here, GROUP + 2, HDIM)
    angles = token_angles(lengths, offsets, first_token, per_device, HDIM)
    queries = rotate(projected[:, :, :GROUP].reshape(per_device, heads_here * GROUP, HDIM), angles)
    queries = queries.astype(jnp.bfloat16).reshape(per_device, heads_here, GROUP, HDIM)
    new_keys = rotate(projected[:, :, GROUP], angles).astype(jnp.bfloat16)
    new_values = projected[:, :, GROUP + 1].astype(jnp.bfloat16)
    new_cache = jnp.stack([new_keys, new_values], axis=2)
    span_all = lax.all_gather(new_cache, "wide", axis=0, tiled=True)
    my_tokens = first_token + jnp.arange(per_device, dtype=jnp.int32)
    my_requests = my_tokens % R
    owned_any = jnp.any(
        my_requests[:, None] == jnp.arange(lengths.shape[0], dtype=jnp.int32)[None, :], axis=0
    )
    furthest = jnp.max(jnp.where(owned_any, lengths, 0))
    remote = lax.all_gather(cache_kv, "wide", axis=1, tiled=True)
    running = lax.cond(
        jnp.int32(0) < furthest,
        lambda state: cache_step(state, remote, queries, my_requests, lengths),
        lambda state: state,
        start_state(per_device, heads_here),
    )
    token_all = jnp.arange(all_tokens, dtype=jnp.int32)
    span_allowed = ((token_all % R)[None, :] == my_requests[:, None]) & (
        token_all[None, :] <= my_tokens[:, None]
    )
    span_scores = (
        jnp.einsum("thgd,shd->thgs", queries, span_all[:, :, 0], preferred_element_type=jnp.float32)
        * score_scale
    )
    peak, weight_sum, accumulated = absorb(
        running, span_scores, span_allowed[:, None, None, :], span_all[:, :, 1], "thgs,shd->thgd"
    )
    attended = (accumulated / weight_sum[..., None]).astype(jnp.bfloat16).reshape(per_device, -1)
    softmax_sums = (peak + jnp.log(weight_sum)).reshape(per_device, -1)
    attn_partial = jnp.dot(
        lax.all_gather(attended, "wide", axis=0, tiled=True),
        w_out,
        preferred_element_type=jnp.float32,
    )
    residual = (hidden_in.astype(jnp.float32) + narrow_sums(attn_partial)).astype(jnp.bfloat16)
    normed_mlp = norm_block(residual, mlp_gain)
    flat_gate_up = w_gate_up.reshape(w_gate_up.shape[0], -1)
    unit_count = w_gate_up.shape[2]
    row_block = normed_mlp
    summed = lax.psum_scatter(
        jnp.dot(row_block, flat_gate_up, preferred_element_type=jnp.float32),
        "wide",
        scatter_dimension=0,
        tiled=True,
    ).reshape(per_device, 2, unit_count)
    hidden = (jax.nn.silu(summed[:, 0]) * summed[:, 1]).astype(jnp.bfloat16)
    mlp_partial = jnp.dot(
        lax.all_gather(hidden, "wide", axis=0, tiled=True),
        w_down,
        preferred_element_type=jnp.float32,
    )
    hidden_out = (residual.astype(jnp.float32) + narrow_sums(mlp_partial)).astype(jnp.bfloat16)
    return (hidden_out, softmax_sums, new_cache)


def solution(mesh):
    return jax.shard_map(
        local,
        mesh=mesh,
        in_specs=(
            P(None, ("wide", "narrow")),
            P(("wide", "narrow")),
            P("wide", "narrow", None),
            P(None, "wide", "narrow", None, None),
            P(),
            P(),
            P("narrow", "wide"),
            P(("wide", "narrow")),
            P("wide", None, "narrow"),
            P("narrow", "wide"),
        ),
        out_specs=(
            P(None, ("wide", "narrow")),
            P("wide", "narrow"),
            P("wide", "narrow", None, None),
        ),
        check_vma=False,
    )
```

profile of v0, /device:TPU:0, one launch (start us, length us, event | category | flops | bytes accessed | tf_op | source)
XLA Modules:
  0.0 629.7 jit_solution(1078234093537580694)
XLA Ops:
  7.2 0.0 reduce-scatter.5.cloned.1.call-start
  7.2 1.4 dynamic-slice
  9.3 0.9 dynamic-update-slice
  10.2 0.8 dynamic-update-slice.1
  11.0 14.7 %all-reduce.2 = (bf16[448]{0:T(512)(128)(2,1)S(1)}, bf16[448]{0:T(512)(128)(2,1)S(1)}) all-reduce(bf16[448]{0:T(512)(128)(2,1)S(1)} %dynamic-update-slice, bf16[448]{0:T(512)(128)(2,1)S(1)} %dynamic-update-slice.1), channel_id=2, replica_groups=mesh['wide'=16,'narrow'=8] {'narrow'}, use_global_device_ids=true, to_apply=%add | all-reduce | flops 896 | bytes 3584
  25.7 13.8 %all_gather.25 = bf16[1024,448]{0,1:T(8,128)(2,1)S(1)} all-gather(bf16[1024,56]{0,1:T(8,128)(2,1)} %param.12), channel_id=1, replica_groups=mesh['wide'=16,'narrow'=8] {'narrow'}, dimensions={1}, use_global_device_ids=true | all-gather | bytes 1032192 | tf_op jit(solution)/shard_map/all_gather | solution.py:17
  39.5 0.2 fusion.32
  39.7 41.9 %psum.14 = f32[1024]{0:T(1024)S(1)} all-reduce(f32[1024]{0:T(1024)S(1)} %fusion.32), channel_id=1, replica_groups=mesh['wide'=16,'narrow'=8] {'wide'}, use_global_device_ids=true, to_apply=%region_3.4 | all-reduce | flops 1024 | bytes 8192 | tf_op jit(solution)/shard_map/psum | solution.py:21
  81.7 5.0 fusion.44
  86.7 0.0 reduce-scatter.5.cloned.1.call-update
  86.7 0.0 all-gather.6.cloned.1.call-start
  86.8 0.9 copy-done.3
  87.6 0.7 copy.28
  88.4 0.0 all-gather.6.cloned.1.call-update
  88.4 0.0 all-gather.8.cloned.1.call-start
  88.5 0.1 fusion.81
  88.6 0.6 select_reduce_fusion.1
  89.9 0.1 select_reduce_fusion
  90.0 0.2 multiply_cosine_fusion.1
  90.2 0.1 fusion.62
  90.4 69.7 %reduce-scatter.5.cloned.1.call-done = f32[64,1152]{1,0:T(8,128)} async-done(((f32[1024,1152]{1,0:T(8,128)}), f32[64,1152]{1,0:T(8,128)}) %reduce-scatter.5.cloned.1.call-update) | async-done | bytes 294928 | tf_op jit(solution)/shard_map/reduce_scatter | solution.py:104
  160.0 1.0 reshape.470
  161.2 0.2 fusion.75
  161.4 0.1 pad_maximum_fusion.1
  161.5 0.1 subtract_convert_fusion
  161.6 0.1 pad_maximum_fusion
  161.8 23.7 %all_gather.27 = bf16[1024,1,2,128]{3,0,2,1:T(8,128)(2,1)S(1)} all-gather(bf16[64,1,2,128]{3,0,2,1:T(8,128)(2,1)S(1)} %pad_maximum_fusion.1), channel_id=1, replica_groups=mesh['wide'=16,'narrow'=8] {'wide'}, dimensions={0}, use_global_device_ids=true | all-gather | bytes 557056 | tf_op jit(solution)/shard_map/all_gather | solution.py:117
  185.5 1.7 fusion.38
  187.2 26.8 %all-gather.6.cloned.1.call-done = bf16[2,4096,1,2,128]{4,1,0,3,2:T(8,128)(2,1)} async-done(((bf16[2,256,1,2,128]{4,1,0,3,2:T(8,128)(2,1)}), bf16[2,4096,1,2,128]{4,1,0,3,2:T(8,128)(2,1)}) %all-gather.6.cloned.1.call-update) | async-done | bytes 4194320 | tf_op jit(solution)/shard_map/all_gather | solution.py:124
  214.0 23.4 %conditional.1 = (f32[64,1,7]{0,2,1:T(8,128)S(1)}, f32[64,1,7]{0,2,1:T(8,128)S(1)}, f32[64,1,7,128]{3,0,2,1:T(8,128)S(1)}) conditional(s32[]{:T(128)} %convert_element_type.73, () %tuple.19, (s32[64]{0:T(128)S(1)}, s32[64]{0:T(128)S(1)}, s32[2]{0:T(128)S(1)}, bf16[2,4096,1,2,128]{4,1,0,3,2:T(8,128)(2,1)}, bf16[64,1,7,128]{3,0,2,1:T(8,128)(2,1)S(1)}) %tuple.52), branch_computations={%region_6.7_spmd, %region_7.10_spmd} | conditional | flops 1927350912 | bytes 126217040 | solution.py:125
  214.0 0.1 iota_compare_fusion
  214.1 0.3 broadcast_and_fusion
  214.5 4.3 fusion
  218.8 5.2 copy-done.1
  224.0 3.9 fusion.22
  227.9 9.5 %fusion.2 = f32[64,7]{0,1:T(8,128)S(1)} fusion(f32[2,4096,64,7]{1,2,3,0:T(8,128)} %copy-done.1, f32[64,7]{0,1:T(8,128)S(1)} %get-tuple-element.67, pred[64,2,4096]{2,0,1:T(8,128)(4,1)S(1)} %broadcast_and_fusion), kind=kLoop, calls=%fused_computation.4 | loop fusion | flops 18349632 | bytes 15207936 | tf_op jit(solution)/shard_map/cond/branch_1_fun/reduce_sum | solution.py:64
  237.4 2.1 fusion.39
  239.5 0.6 add_bitcast_fusion
  240.1 2.1 fusion.43
  242.2 0.1 copy.32
  242.3 0.7 copy.54
  243.0 0.0 all-gather.8.cloned.1.call-update
  243.0 0.3 reduce-scatter.7.cloned.1.call-start
  243.3 44.3 %all-gather.8.cloned.1.call-done = bf16[1024,896]{1,0:T(8,128)(2,1)} async-done(((bf16[64,896]{1,0:T(8,128)(2,1)}), bf16[1024,896]{1,0:T(8,128)(2,1)}) %all-gather.8.cloned.1.call-update) | async-done | bytes 1835024 | tf_op jit(solution)/shard_map/all_gather | solution.py:145
  287.5 4.1 fusion.89
  291.6 0.0 reduce-scatter.9.cloned.1.call-start
  291.7 5.5 copy.43
  297.2 27.0 %reduce-scatter.7.cloned.1.call-done = f32[1024,56]{0,1:T(8,128)} async-done(((f32[1024,448]{0,1:T(8,128)}), f32[1024,56]{0,1:T(8,128)}) %reduce-scatter.7.cloned.1.call-update) | async-done | bytes 229392 | tf_op jit(solution)/shard_map/reduce_scatter | solution.py:27
  324.1 1.0 add_convert_fusion.1
  325.1 13.6 %all_gather.29 = bf16[1024,448]{0,1:T(8,128)(2,1)S(1)} all-gather(bf16[1024,56]{0,1:T(8,128)(2,1)S(1)} %add_convert_fusion.1), channel_id=1, replica_groups=mesh['wide'=16,'narrow'=8] {'narrow'}, dimensions={1}, use_global_device_ids=true | all-gather | bytes 1032192 | tf_op jit(solution)/shard_map/all_gather | solution.py:17
  338.7 0.2 fusion.35
  338.9 40.6 %psum.15 = f32[1024]{0:T(1024)S(1)} all-reduce(f32[1024]{0:T(1024)S(1)} %fusion.35), channel_id=1, replica_groups=mesh['wide'=16,'narrow'=8] {'wide'}, use_global_device_ids=true, to_apply=%region_14.15 | all-reduce | flops 1024 | bytes 8192 | tf_op jit(solution)/shard_map/psum | solution.py:21
  379.5 12.3 %fusion.48 = f32[1024,5120]{1,0:T(8,128)} fusion(bf16[448,5120]{1,0:T(8,128)(2,1)} %bitcast.180, bf16[1024,448]{0,1:T(8,128)(2,1)S(1)} %all_gather.29, f32[448]{0:T(512)S(1)} %mul.228, f32[1024]{0:T(1024)S(1)} %add_rsqrt_fusion), kind=kOutput, calls=%fused_computation.50 | convolution fusion | flops 4699455488 | bytes 26482432 | tf_op jit(solution)/shard_map/dot_general | solution.py:155
  391.9 0.0 all-gather.10.cloned.1.call-start
  391.9 126.7 %reduce-scatter.9.cloned.1.call-done = f32[64,5120]{1,0:T(8,128)} async-done(((f32[1024,5120]{1,0:T(8,128)}), f32[64,5120]{1,0:T(8,128)}) %reduce-scatter.9.cloned.1.call-update) | async-done | bytes 1310736 | tf_op jit(solution)/shard_map/reduce_scatter | solution.py:154
  518.6 3.3 reshape.478
  522.0 2.9 fusion.88
  524.8 0.9 fusion.60
  525.8 0.0 reduce-scatter.11.cloned.1.call-start
  525.8 56.2 %all-gather.10.cloned.1.call-done = bf16[1024,2560]{1,0:T(8,128)(2,1)} async-done(((bf16[64,2560]{1,0:T(8,128)(2,1)}), bf16[1024,2560]{1,0:T(8,128)(2,1)}) %all-gather.10.cloned.1.call-update) | async-done | bytes 5242896 | tf_op jit(solution)/shard_map/all_gather | solution.py:162
  582.0 6.3 %fusion.90 = f32[1024,448]{0,1:T(8,128)} fusion(bf16[1024,2560]{1,0:T(8,128)(2,1)} %all-gather.10.cloned.1.call-done, bf16[2560,448]{0,1:T(8,128)(2,1)S(1)} %copy-done), kind=kOutput, calls=%fused_computation.127 | convolution fusion | flops 2348810240 | bytes 9371648 | tf_op jit(solution)/shard_map/dot_general | solution.py:161
  588.4 0.6 copy.34
  589.0 32.2 %reduce-scatter.11.cloned.1.call-done = f32[1024,56]{0,1:T(8,128)} async-done(((f32[1024,448]{0,1:T(8,128)}), f32[1024,56]{0,1:T(8,128)}) %reduce-scatter.11.cloned.1.call-update) | async-done | bytes 229392 | tf_op jit(solution)/shard_map/reduce_scatter | solution.py:27
  621.2 1.6 add_convert_fusion
  (40 shorter events, 0.3 us)
Async XLA Ops:
  7.2 574.9 %copy-start = (bf16[2560,448]{0,1:T(8,128)(2,1)S(1)}, bf16[2560,448]{0,1:T(8,128)(2,1)}, u32[]{:S(2)}) copy-start(bf16[2560,448]{0,1:T(8,128)(2,1)} %param.21) | copy-start | bytes 6881284
  7.2 152.9 %reduce-scatter.5.cloned.1.call-start = ((), (), s32[]{:S(2)}) async-start(), calls=%async_computation.5 | async-start | bytes 5013504 | tf_op jit(solution)/shard_map/reduce_scatter | solution.py:104
  86.7 0.9 copy-start.3
  86.7 1.9 copy-start.4
  86.7 1.9 copy-start.5
  86.7 127.3 %all-gather.6.cloned.1.call-start = ((), (), s32[]{:S(2)}) async-start(), calls=%async_computation.4 | async-start | bytes 4456448 | tf_op jit(solution)/shard_map/all_gather | solution.py:124
  88.4 199.1 %all-gather.8.cloned.1.call-start = ((), (), s32[]{:S(2)}) async-start(), calls=%async_computation.6 | async-start | bytes 1949696 | tf_op jit(solution)/shard_map/all_gather | solution.py:145
  214.5 9.5 %copy-start.6 = (bf16[2,4096,1,2,128]{4,1,0,3,2:T(8,128)(2,1)S(1)}, bf16[2,4096,1,2,128]{4,1,0,3,2:T(8,128)(2,1)}, u32[]{:S(2)}) copy-start(bf16[2,4096,1,2,128]{4,1,0,3,2:T(8,128)(2,1)} %get-tuple-element.42) | copy-start | bytes 12582916 | tf_op jit(solution)/shard_map/cond
  218.8 5.2 copy-start.1
  243.0 81.1 %reduce-scatter.7.cloned.1.call-start = ((), (), s32[]{:S(2)}) async-start(), calls=%async_computation.7 | async-start | bytes 2064384 | tf_op jit(solution)/shard_map/reduce_scatter | solution.py:27
  291.6 227.0 %reduce-scatter.9.cloned.1.call-start = ((), (), s32[]{:S(2)}) async-start(), calls=%async_computation.8 | async-start | bytes 22282240 | tf_op jit(solution)/shard_map/reduce_scatter | solution.py:154
  291.7 32.4 %copy-start.2 = (bf16[1024,56]{0,1:T(8,128)(2,1)S(1)}, bf16[1024,56]{0,1:T(8,128)(2,1)}, u32[]{:S(2)}) copy-start(bf16[1024,56]{0,1:T(8,128)(2,1)} %param.12) | copy-start | bytes 344068
  391.9 190.2 %all-gather.10.cloned.1.call-start = ((), (), s32[]{:S(2)}) async-start(), calls=%async_computation.9 | async-start | bytes 5570560 | tf_op jit(solution)/shard_map/all_gather | solution.py:162
  525.8 95.5 %reduce-scatter.11.cloned.1.call-start = ((), (), s32[]{:S(2)}) async-start(), calls=%async_computation.10 | async-start | bytes 2064384 | tf_op jit(solution)/shard_map/reduce_scatter | solution.py:27
Sparse Core Ops, SparseCore 0:
  86.8 73.1 reduce-scatter.4
  162.2 51.7 all-gather.5
  243.1 44.3 all-gather.7
  291.8 32.3 reduce-scatter.6
  392.0 126.6 reduce-scatter.8
  525.9 56.1 all-gather.9
  588.5 32.6 reduce-scatter.10
where the time goes:
time: 630 us
  waiting for transfers between devices  383 us (61%)
  blocking collectives  148 us (23%)
  matrix products  39.7 us (6%)
  local copies, waits for them, and re-layouts  24.1 us (4%)
  other arithmetic  18.3 us (3%)
  between operations  15.6 us (2%)
    reduce_scatter x1, waiting for transfers between devices, local(): lax.psum_scatter(jnp.dot(row_block, flat_gate_up, preferred_element_type=...  127 us
    psum x2, blocking collectives, norm_block(): squares = lax.psum(jnp.sum(widened * widened, axis=1), 'wide')  82.5 us
    reduce_scatter x1, waiting for transfers between devices, local(): lax.psum_scatter(jnp.dot(row_block, flat_qkv, preferred_element_type=jnp....  69.7 us
    reduce_scatter x2, waiting for transfers between devices, narrow_sums(): lax.psum_scatter(partial_value, 'narrow', scatter_dimension=1, tiled=True)  59.2 us
    all_gather x1, waiting for transfers between devices, local(): lax.all_gather(hidden, 'wide', axis=0, tiled=True)  56.2 us
    all_gather x1, waiting for transfers between devices, local(): lax.all_gather(attended, 'wide', axis=0, tiled=True)  44.3 us
    all_gather x2, blocking collectives, norm_block(): lax.all_gather(values, 'narrow', axis=1, tiled=True)  27.4 us
    all_gather x1, waiting for transfers between devices, local(): remote = lax.all_gather(cache_kv, 'wide', axis=1, tiled=True)  26.8 us
  transfers between devices with their start and end apart: 7, of which 7 were waited for; matrix products, arithmetic and copies ran while one was open for 2% of the time, Pallas kernels for 0%

commit v1 on v0

--- a/solution.py
+++ b/solution.py
@@ -18,7 +18,7 @@
         lax.all_gather(gain_vec.reshape(1, -1), "narrow", axis=1, tiled=True),
     )
     widened = gathered.astype(jnp.float32)
-    squares = lax.psum(jnp.sum(widened * widened, axis=1), "wide")
+    squares = jnp.sum(lax.all_gather(jnp.sum(widened * widened, axis=1), "wide"), axis=0)
     inv_scale = lax.rsqrt(squares / D + epsilon)
     return (widened * inv_scale[:, None] * gain_row.astype(jnp.float32)).astype(jnp.bfloat16)
 

time: 630 us -> 603 us (0.957)
  blocking collectives: 148 us -> 115 us
    psum x2 -> x0, blocking collectives: 82.5 us -> none  [norm_block(): squares = lax.psum(jnp.sum(widened * widened, axis=1), 'wide')]
    all_gather x0 -> x2, blocking collectives: none -> 49 us  [norm_block(): lax.all_gather(jnp.sum(widened * widened, axis=1), 'wide')]
where the time goes in v1:
time: 603 us; the launch traced here: 602 us
  waiting for transfers between devices  389 us (65%)
  blocking collectives  115 us (19%)
  matrix products  39.7 us (7%)
  local copies, waits for them, and re-layouts  24.1 us (4%)
  other arithmetic  18.3 us (3%)
  between operations  15.7 us (3%)
    reduce_scatter x1, waiting for transfers between devices, local(): lax.psum_scatter(jnp.dot(row_block, flat_gate_up, preferred_element_type=...  129 us
    reduce_scatter x1, waiting for transfers between devices, local(): lax.psum_scatter(jnp.dot(row_block, flat_qkv, preferred_element_type=jnp....  72.8 us
    reduce_scatter x2, waiting for transfers between devices, narrow_sums(): lax.psum_scatter(partial_value, 'narrow', scatter_dimension=1, tiled=True)  59.2 us
    all_gather x1, waiting for transfers between devices, local(): lax.all_gather(hidden, 'wide', axis=0, tiled=True)  56.2 us
    all_gather x2, blocking collectives, norm_block(): lax.all_gather(jnp.sum(widened * widened, axis=1), 'wide')  49 us
    all_gather x1, waiting for transfers between devices, local(): lax.all_gather(attended, 'wide', axis=0, tiled=True)  44.3 us
    all_gather x2, blocking collectives, norm_block(): lax.all_gather(values, 'narrow', axis=1, tiled=True)  27.4 us
    all_gather x1, waiting for transfers between devices, local(): remote = lax.all_gather(cache_kv, 'wide', axis=1, tiled=True)  26.8 us
  transfers between devices with their start and end apart: 7, of which 7 were waited for; matrix products, arithmetic and copies ran while one was open for 2% of the time, Pallas kernels for 0%

profile of v1, /device:TPU:0, one launch (start us, length us, event | category | flops | bytes accessed | tf_op | source)
XLA Modules:
  0.0 602.1 jit_solution(7634712696827236631)
XLA Ops:
  7.2 0.0 reduce-scatter.5.cloned.1.call-start
  7.2 1.4 dynamic-slice
  9.3 0.9 dynamic-update-slice
  10.2 0.8 dynamic-update-slice.1
  11.0 14.7 %all-reduce.2 = (bf16[448]{0:T(512)(128)(2,1)S(1)}, bf16[448]{0:T(512)(128)(2,1)S(1)}) all-reduce(bf16[448]{0:T(512)(128)(2,1)S(1)} %dynamic-update-slice, bf16[448]{0:T(512)(128)(2,1)S(1)} %dynamic-update-slice.1), channel_id=3, replica_groups=mesh['wide'=16,'narrow'=8] {'narrow'}, use_global_device_ids=true, to_apply=%add | all-reduce | flops 896 | bytes 3584
  25.7 13.8 %all_gather.37 = bf16[1024,448]{0,1:T(8,128)(2,1)S(1)} all-gather(bf16[1024,56]{0,1:T(8,128)(2,1)} %param.12), channel_id=1, replica_groups=mesh['wide'=16,'narrow'=8] {'narrow'}, dimensions={1}, use_global_device_ids=true | all-gather | bytes 1032192 | tf_op jit(solution)/shard_map/all_gather | solution.py:17
  39.5 0.2 fusion.32
  39.7 25.2 %all-gather = f32[16384]{0:T(1024)S(1)} all-gather(f32[1024]{0:T(1024)S(1)} %fusion.32), channel_id=2, replica_groups=mesh['wide'=16,'narrow'=8] {'wide'}, dimensions={0}, use_global_device_ids=true | all-gather | bytes 69632 | tf_op jit(solution)/shard_map/all_gather | solution.py:21
  65.0 5.0 fusion.44
  70.0 0.0 reduce-scatter.5.cloned.1.call-update
  70.0 0.0 all-gather.8.cloned.1.call-start
  70.0 0.9 copy-done.3
  70.9 0.7 copy.35
  71.6 0.0 all-gather.8.cloned.1.call-update
  71.7 0.0 all-gather.10.cloned.1.call-start
  71.7 0.1 fusion.81
  71.9 0.6 select_reduce_fusion.1
  73.2 0.1 select_reduce_fusion
  73.3 0.2 multiply_cosine_fusion.1
  73.5 0.1 fusion.62
  73.6 72.8 %reduce-scatter.5.cloned.1.call-done = f32[64,1152]{1,0:T(8,128)} async-done(((f32[1024,1152]{1,0:T(8,128)}), f32[64,1152]{1,0:T(8,128)}) %reduce-scatter.5.cloned.1.call-update) | async-done | bytes 294928 | tf_op jit(solution)/shard_map/reduce_scatter | solution.py:104
  146.4 1.0 reshape.478
  147.6 0.2 fusion.75
  147.8 0.1 pad_maximum_fusion.1
  147.9 0.1 subtract_convert_fusion
  148.0 0.1 pad_maximum_fusion
  148.1 23.7 %all_gather.41 = bf16[1024,1,2,128]{3,0,2,1:T(8,128)(2,1)S(1)} all-gather(bf16[64,1,2,128]{3,0,2,1:T(8,128)(2,1)S(1)} %pad_maximum_fusion.1), channel_id=1, replica_groups=mesh['wide'=16,'narrow'=8] {'wide'}, dimensions={0}, use_global_device_ids=true | all-gather | bytes 557056 | tf_op jit(solution)/shard_map/all_gather | solution.py:117
  171.9 1.7 fusion.38
  173.6 26.8 %all-gather.8.cloned.1.call-done = bf16[2,4096,1,2,128]{4,1,0,3,2:T(8,128)(2,1)} async-done(((bf16[2,256,1,2,128]{4,1,0,3,2:T(8,128)(2,1)}), bf16[2,4096,1,2,128]{4,1,0,3,2:T(8,128)(2,1)}) %all-gather.8.cloned.1.call-update) | async-done | bytes 4194320 | tf_op jit(solution)/shard_map/all_gather | solution.py:124
  200.4 23.4 %conditional.1 = (f32[64,1,7]{0,2,1:T(8,128)S(1)}, f32[64,1,7]{0,2,1:T(8,128)S(1)}, f32[64,1,7,128]{3,0,2,1:T(8,128)S(1)}) conditional(s32[]{:T(128)} %convert_element_type.73, () %tuple.19, (s32[64]{0:T(128)S(1)}, s32[64]{0:T(128)S(1)}, s32[2]{0:T(128)S(1)}, bf16[2,4096,1,2,128]{4,1,0,3,2:T(8,128)(2,1)}, bf16[64,1,7,128]{3,0,2,1:T(8,128)(2,1)S(1)}) %tuple.53), branch_computations={%region_6.7_spmd, %region_7.10_spmd} | conditional | flops 1927350912 | bytes 126217040 | solution.py:125
  200.4 0.1 iota_compare_fusion
  200.5 0.3 broadcast_and_fusion
  200.8 4.3 fusion
  205.2 5.2 copy-done.1
  210.4 3.9 fusion.22
  214.3 9.5 %fusion.2 = f32[64,7]{0,1:T(8,128)S(1)} fusion(f32[2,4096,64,7]{1,2,3,0:T(8,128)} %copy-done.1, f32[64,7]{0,1:T(8,128)S(1)} %get-tuple-element.70, pred[64,2,4096]{2,0,1:T(8,128)(4,1)S(1)} %broadcast_and_fusion), kind=kLoop, calls=%fused_computation.4 | loop fusion | flops 18349632 | bytes 15207936 | tf_op jit(solution)/shard_map/cond/branch_1_fun/reduce_sum | solution.py:64
  223.8 2.1 fusion.39
  225.8 0.6 add_bitcast_fusion
  226.5 2.1 fusion.43
  228.6 0.1 copy.39
  228.7 0.7 copy.61
  229.3 0.0 all-gather.10.cloned.1.call-update
  229.4 0.3 reduce-scatter.7.cloned.1.call-start
  229.6 44.3 %all-gather.10.cloned.1.call-done = bf16[1024,896]{1,0:T(8,128)(2,1)} async-done(((bf16[64,896]{1,0:T(8,128)(2,1)}), bf16[1024,896]{1,0:T(8,128)(2,1)}) %all-gather.10.cloned.1.call-update) | async-done | bytes 1835024 | tf_op jit(solution)/shard_map/all_gather | solution.py:145
  273.9 4.1 fusion.89
  278.0 0.0 reduce-scatter.9.cloned.1.call-start
  278.1 5.5 copy.50
  283.5 27.0 %reduce-scatter.7.cloned.1.call-done = f32[1024,56]{0,1:T(8,128)} async-done(((f32[1024,448]{0,1:T(8,128)}), f32[1024,56]{0,1:T(8,128)}) %reduce-scatter.7.cloned.1.call-update) | async-done | bytes 229392 | tf_op jit(solution)/shard_map/reduce_scatter | solution.py:27
  310.5 1.0 add_convert_fusion.1
  311.5 13.6 %all_gather.43 = bf16[1024,448]{0,1:T(8,128)(2,1)S(1)} all-gather(bf16[1024,56]{0,1:T(8,128)(2,1)S(1)} %add_convert_fusion.1), channel_id=1, replica_groups=mesh['wide'=16,'narrow'=8] {'narrow'}, dimensions={1}, use_global_device_ids=true | all-gather | bytes 1032192 | tf_op jit(solution)/shard_map/all_gather | solution.py:17
  325.1 0.2 fusion.35
  325.3 23.9 %all-gather.2 = f32[16384]{0:T(1024)S(1)} all-gather(f32[1024]{0:T(1024)S(1)} %fusion.35), channel_id=4, replica_groups=mesh['wide'=16,'narrow'=8] {'wide'}, dimensions={0}, use_global_device_ids=true | all-gather | bytes 69632 | tf_op jit(solution)/shard_map/all_gather | solution.py:21
  349.2 12.3 %fusion.48 = f32[1024,5120]{1,0:T(8,128)} fusion(bf16[448,5120]{1,0:T(8,128)(2,1)} %bitcast.180, bf16[1024,448]{0,1:T(8,128)(2,1)S(1)} %all_gather.43, f32[448]{0:T(512)S(1)} %mul.228, f32[1024]{0:T(1024)S(1)} %add_rsqrt_fusion), kind=kOutput, calls=%fused_computation.50 | convolution fusion | flops 4699455488 | bytes 26482432 | tf_op jit(solution)/shard_map/dot_general | solution.py:155
  361.5 0.0 all-gather.12.cloned.1.call-start
  361.6 129.4 %reduce-scatter.9.cloned.1.call-done = f32[64,5120]{1,0:T(8,128)} async-done(((f32[1024,5120]{1,0:T(8,128)}), f32[64,5120]{1,0:T(8,128)}) %reduce-scatter.9.cloned.1.call-update) | async-done | bytes 1310736 | tf_op jit(solution)/shard_map/reduce_scatter | solution.py:154
  491.0 3.3 reshape.486
  494.3 2.9 fusion.88
  497.2 0.9 fusion.60
  498.1 0.0 reduce-scatter.11.cloned.1.call-start
  498.2 56.2 %all-gather.12.cloned.1.call-done = bf16[1024,2560]{1,0:T(8,128)(2,1)} async-done(((bf16[64,2560]{1,0:T(8,128)(2,1)}), bf16[1024,2560]{1,0:T(8,128)(2,1)}) %all-gather.12.cloned.1.call-update) | async-done | bytes 5242896 | tf_op jit(solution)/shard_map/all_gather | solution.py:162
  554.4 6.3 %fusion.90 = f32[1024,448]{0,1:T(8,128)} fusion(bf16[1024,2560]{1,0:T(8,128)(2,1)} %all-gather.12.cloned.1.call-done, bf16[2560,448]{0,1:T(8,128)(2,1)S(1)} %copy-done), kind=kOutput, calls=%fused_computation.127 | convolution fusion | flops 2348810240 | bytes 9371648 | tf_op jit(solution)/shard_map/dot_general | solution.py:161
  560.8 0.6 copy.41
  561.4 32.2 %reduce-scatter.11.cloned.1.call-done = f32[1024,56]{0,1:T(8,128)} async-done(((f32[1024,448]{0,1:T(8,128)}), f32[1024,56]{0,1:T(8,128)}) %reduce-scatter.11.cloned.1.call-update) | async-done | bytes 229392 | tf_op jit(solution)/shard_map/reduce_scatter | solution.py:27
  593.6 1.6 add_convert_fusion
  (44 shorter events, 0.4 us)
Async XLA Ops:
  7.2 547.3 %copy-start = (bf16[2560,448]{0,1:T(8,128)(2,1)S(1)}, bf16[2560,448]{0,1:T(8,128)(2,1)}, u32[]{:S(2)}) copy-start(bf16[2560,448]{0,1:T(8,128)(2,1)} %param.21) | copy-start | bytes 6881284
  7.2 139.2 %reduce-scatter.5.cloned.1.call-start = ((), (), s32[]{:S(2)}) async-start(), calls=%async_computation.5 | async-start | bytes 5013504 | tf_op jit(solution)/shard_map/reduce_scatter | solution.py:104
  69.9 0.9 copy-start.3
  70.0 1.9 copy-start.4
  70.0 1.9 copy-start.5
  70.0 130.4 %all-gather.8.cloned.1.call-start = ((), (), s32[]{:S(2)}) async-start(), calls=%async_computation.4 | async-start | bytes 4456448 | tf_op jit(solution)/shard_map/all_gather | solution.py:124
  71.7 202.2 %all-gather.10.cloned.1.call-start = ((), (), s32[]{:S(2)}) async-start(), calls=%async_computation.6 | async-start | bytes 1949696 | tf_op jit(solution)/shard_map/all_gather | solution.py:145
  200.8 9.5 %copy-start.6 = (bf16[2,4096,1,2,128]{4,1,0,3,2:T(8,128)(2,1)S(1)}, bf16[2,4096,1,2,128]{4,1,0,3,2:T(8,128)(2,1)}, u32[]{:S(2)}) copy-start(bf16[2,4096,1,2,128]{4,1,0,3,2:T(8,128)(2,1)} %get-tuple-element.42) | copy-start | bytes 12582916 | tf_op jit(solution)/shard_map/cond
  205.2 5.2 copy-start.1
  229.4 81.1 %reduce-scatter.7.cloned.1.call-start = ((), (), s32[]{:S(2)}) async-start(), calls=%async_computation.7 | async-start | bytes 2064384 | tf_op jit(solution)/shard_map/reduce_scatter | solution.py:27
  278.0 213.0 %reduce-scatter.9.cloned.1.call-start = ((), (), s32[]{:S(2)}) async-start(), calls=%async_computation.8 | async-start | bytes 22282240 | tf_op jit(solution)/shard_map/reduce_scatter | solution.py:154
  278.1 32.4 %copy-start.2 = (bf16[1024,56]{0,1:T(8,128)(2,1)S(1)}, bf16[1024,56]{0,1:T(8,128)(2,1)}, u32[]{:S(2)}) copy-start(bf16[1024,56]{0,1:T(8,128)(2,1)} %param.12) | copy-start | bytes 344068
  361.5 192.9 %all-gather.12.cloned.1.call-start = ((), (), s32[]{:S(2)}) async-start(), calls=%async_computation.9 | async-start | bytes 5570560 | tf_op jit(solution)/shard_map/all_gather | solution.py:162
  498.1 95.5 %reduce-scatter.11.cloned.1.call-start = ((), (), s32[]{:S(2)}) async-start(), calls=%async_computation.10 | async-start | bytes 2064384 | tf_op jit(solution)/shard_map/reduce_scatter | solution.py:27
Sparse Core Ops, SparseCore 0:
  70.1 76.2 reduce-scatter.4
  148.6 51.7 all-gather.7
  229.5 44.3 all-gather.9
  278.1 32.3 reduce-scatter.6
  361.7 129.3 reduce-scatter.8
  498.3 56.1 all-gather.11
  560.9 32.6 reduce-scatter.10
